TPU v7x, 32 devices: a whole 2x2x4 slice. The times are simulated.
32 devices in a mesh: ctx: 4 (over y, x), exp: 8 (over z, core).
Axes of the slice: x: 2, y: 2, z: 4, core: 2. Of those that a mesh axis runs over, the one named last changes fastest.
Arguments:
- inputs: bfloat16 [4, 6144, 768], P('ctx', 'exp'), may hold values from -6 to 6
- prev_logits: float32 [4, 6144, 12], P('ctx', 'exp'), may hold values from -4 to 4
- routes: int32 [4, 6144, 2], P('ctx', 'exp'), may hold values from 0 to 11, all different within a row; in each aligned block of 768 rows (0 to 767, 768 to 1535, ..., all dimensions but the last counted through in order) at most 144 rows name the same one
- attn_gain: float32 [768], replicated, may hold values from 0.25 to 1.75
- w_qkv: bfloat16 [768, 2304], replicated, may hold values from -0.21875 to 0.21875
- w_out: bfloat16 [768, 768], replicated, may hold values from -0.875 to 0.875
- moe_gain: float32 [768], replicated, may hold values from 0.25 to 1.75
- router: bfloat16 [768, 12], replicated, may hold values from -0.109375 to 0.109375
- const_gate: bfloat16 [2, 768, 2], replicated, may hold values from -0.21875 to 0.21875
- const_vec: float32 [2, 768], replicated, may hold values from -12 to 12
- w_gate: bfloat16 [8, 768, 2048], P('exp'), may hold values from -0.21875 to 0.21875
- w_up: bfloat16 [8, 768, 2048], P('exp'), may hold values from -0.21875 to 0.21875
- w_down: bfloat16 [8, 2048, 768], P('exp'), may hold values from -1.5 to 1.5
- out_grad: bfloat16 [4, 6144, 768], P('ctx', 'exp'), may hold values from -6 to 6
Outputs:
- mixed_out: bfloat16 [4, 6144, 768], P('ctx', 'exp')
- d_inputs: float32 [4, 6144, 768], P('ctx', 'exp')
- d_prev: float32 [4, 6144, 12], P('ctx', 'exp')
- d_attn_gain: float32 [768], replicated
- d_w_qkv: float32 [768, 2304], replicated
- d_w_out: float32 [768, 768], replicated
- d_moe_gain: float32 [768], replicated
- d_router: float32 [768, 12], replicated
- d_const_gate: float32 [2, 768, 2], replicated
- d_const_vec: float32 [2, 768], replicated
- d_w_gate: float32 [8, 768, 2048], P('exp', 'ctx')
- d_w_up: float32 [8, 768, 2048], P('exp', 'ctx')
- d_w_down: float32 [8, 2048, 768], P('exp', 'ctx')
Inputs may be any that keep to these rules, and one draw needn't show every extreme that they name: `routes`: each row names two different experts. Among the 768 rows of one device no expert is named by more than 144 rows, and on some devices one is named by exactly 144.
All inputs are finite; a program needn't handle non-finite values.
Results may differ from a plain program's by a relative error of at most 0.015.
Values may be sent and summed in bfloat16 or wider, within the bound.
No kernel may reach another device: no remote copies, remote signals or barrier semaphores. Data moves between devices by JAX's collectives and lax.ppermute only.
A program may use at most 256 MiB of HBM per device.

v0:
```python
from functools import partial
import jax
import jax.numpy as jnp
from jax import lax
from jax.sharding import PartitionSpec as P

HEADS = 12
HEAD_DIM = 64
FFN_EXPERTS = 8
ALL_EXPERTS = 12
CONT_LEN = 512
masked_value = -1e30
epsilon = 1e-06
highest = lax.Precision.HIGHEST


def rms_forward(tensor, gain_vec):
    inverse = lax.rsqrt(jnp.mean(tensor * tensor, axis=-1, keepdims=True) + epsilon)
    return (tensor * inverse * gain_vec, inverse)


def rms_backward(tensor, inverse, gain_vec, upstream):
    scaled = upstream * gain_vec
    d_gain = jnp.sum(upstream * tensor * inverse, axis=0)
    d_tensor = inverse * scaled - tensor * inverse**3 * jnp.mean(
        scaled * tensor, axis=-1, keepdims=True
    )
    return (d_tensor, d_gain)


def route_slots(route_rows):
    flat_ids = route_rows.reshape(-1)
    onehot = (flat_ids[:, None] == jnp.arange(ALL_EXPERTS, dtype=jnp.int32)[None, :]).astype(
        jnp.int32
    )
    before = jnp.cumsum(onehot, axis=0) - onehot
    return jnp.sum(before * onehot, axis=1).reshape(route_rows.shape)


def split_heads(tensor):
    reshaped = tensor.reshape(tensor.shape[:-1] + (HEADS, HEAD_DIM))
    return jnp.moveaxis(reshaped, -2, 0)


def join_heads(tensor):
    moved_axes = jnp.moveaxis(tensor, 0, -2)
    return moved_axes.reshape(moved_axes.shape[:-2] + (HEADS * HEAD_DIM,))


def head_forward(allowed, operands):
    queries, key_rows, value_rows = operands
    raw_scores = jnp.einsum(
        "qd,kd->qk", queries, key_rows, preferred_element_type=jnp.float32
    ) * HEAD_DIM ** (-0.5)
    masked = jnp.where(allowed, raw_scores, masked_value)
    row_peak = jnp.max(masked, axis=-1, keepdims=True)
    unnormed = jnp.exp(masked - row_peak)
    row_total = jnp.sum(unnormed, axis=-1, keepdims=True)
    weights_soft = (unnormed / row_total).astype(jnp.bfloat16)
    result = jnp.einsum("qk,kd->qd", weights_soft, value_rows, preferred_element_type=jnp.float32)
    return (result, row_peak[..., 0] + jnp.log(row_total[..., 0]))


def head_backward(allowed, operands):
    queries, key_rows, value_rows, upstream, log_total = operands
    raw_scores = jnp.einsum(
        "qd,kd->qk", queries, key_rows, preferred_element_type=jnp.float32
    ) * HEAD_DIM ** (-0.5)
    masked = jnp.where(allowed, raw_scores, masked_value)
    probs_full = jnp.where(allowed, jnp.exp(masked - log_total[..., None]), 0.0)
    d_values = jnp.einsum(
        "qk,qd->kd", probs_full.astype(jnp.bfloat16), upstream, preferred_element_type=jnp.float32
    )
    d_probs = jnp.einsum("qd,kd->qk", upstream, value_rows, preferred_element_type=jnp.float32)
    d_scores = probs_full * (d_probs - jnp.sum(probs_full * d_probs, axis=-1, keepdims=True))
    d_scores = d_scores.astype(jnp.bfloat16)
    d_queries = jnp.einsum(
        "qk,kd->qd", d_scores, key_rows, preferred_element_type=jnp.float32
    ) * HEAD_DIM ** (-0.5)
    d_keys = jnp.einsum(
        "qk,qd->kd", d_scores, queries, preferred_element_type=jnp.float32
    ) * HEAD_DIM ** (-0.5)
    return (d_queries, d_keys, d_values)


def body(
    inputs,
    prev_logits,
    routes,
    attn_gain,
    w_qkv,
    w_out,
    moe_gain,
    router,
    const_gate,
    const_vec,
    w_gate,
    w_up,
    w_down,
    out_grad,
):
    model_width = inputs.shape[2]
    tok_rows = inputs.shape[1]
    prompt_local = tok_rows - CONT_LEN
    prompt_len = prompt_local * lax.axis_size("ctx")
    split_parts = lax.axis_size("exp") // FFN_EXPERTS
    capacity = max(4, tok_rows // 64 * 12)
    tokens_in = inputs[0].astype(jnp.float32)
    normed_attn, inverse_attn = rms_forward(tokens_in, attn_gain)
    act_low = normed_attn.astype(jnp.bfloat16)
    projected = jnp.dot(act_low, w_qkv, preferred_element_type=jnp.float32).astype(jnp.bfloat16)
    queries = projected[:, :model_width]
    kv_local = projected[:prompt_local, model_width:]
    own_kv = projected[prompt_local:, model_width:]
    gathered = lax.all_gather(kv_local, "ctx", axis=0, tiled=True)
    row_index = jnp.arange(tok_rows, dtype=jnp.int32)
    query_pos = lax.axis_index("ctx") * prompt_local + row_index
    cont_pos = row_index - prompt_local
    key_index = jnp.arange(prompt_len + CONT_LEN, dtype=jnp.int32)
    in_prompt = key_index[None, :] < prompt_len
    prompt_mask = in_prompt & (key_index[None, :] <= query_pos[:, None])
    cont_mask = in_prompt | (key_index[None, :] - prompt_len <= cont_pos[:, None])
    allowed = jnp.where((row_index < prompt_local)[:, None], prompt_mask, cont_mask)
    all_kv = jnp.concatenate([gathered, own_kv], axis=0)
    heads_out, row_lse = lax.map(
        partial(head_forward, allowed),
        (
            split_heads(queries),
            split_heads(all_kv[:, :model_width]),
            split_heads(all_kv[:, model_width:]),
        ),
    )
    mixed_low = join_heads(heads_out).astype(jnp.bfloat16)
    hidden = tokens_in + jnp.dot(mixed_low, w_out, preferred_element_type=jnp.float32)
    normed_moe, inverse_moe = rms_forward(hidden, moe_gain)
    moe_low = normed_moe.astype(jnp.bfloat16)
    logits = jnp.dot(moe_low, router, preferred_element_type=jnp.float32) + prev_logits[0]
    route_ids = routes[0]
    probs_all = jax.nn.softmax(logits, axis=-1)
    gate_values = jnp.take_along_axis(probs_all, route_ids, axis=-1)
    const_logits = jnp.einsum(
        "td,cda->tca", moe_low, const_gate, preferred_element_type=jnp.float32
    )
    alphas = jax.nn.softmax(const_logits, axis=-1)
    const_out = alphas[..., 0:1] * normed_moe[:, None, :] + alphas[..., 1:2] * const_vec[None]
    slot_index = route_slots(route_ids)
    is_ffn = route_ids < FFN_EXPERTS
    expert_ids = jnp.where(is_ffn, route_ids, FFN_EXPERTS)
    token_ids = jnp.broadcast_to(jnp.arange(tok_rows, dtype=jnp.int32)[:, None], route_ids.shape)
    dispatch = (
        jnp.full((FFN_EXPERTS, capacity), tok_rows, jnp.int32)
        .at[expert_ids, slot_index]
        .set(token_ids, mode="drop")
    )
    padded = jnp.concatenate([moe_low, jnp.zeros((1, model_width), jnp.bfloat16)], axis=0)
    dealt = padded[dispatch]
    received = lax.all_to_all(
        jnp.repeat(dealt, split_parts, axis=0), "exp", split_axis=0, concat_axis=0, tiled=True
    )
    leading = received.shape[:2]
    flat_rows = received.reshape(-1, model_width)
    gate_pre = jnp.dot(flat_rows, w_gate[0], preferred_element_type=jnp.float32)
    up_pre = jnp.dot(flat_rows, w_up[0], preferred_element_type=jnp.float32)
    inner_act = (jax.nn.silu(gate_pre) * up_pre).astype(jnp.bfloat16)
    partial_out = jnp.dot(inner_act, w_down[0], preferred_element_type=jnp.float32).astype(
        jnp.bfloat16
    )
    partial_out, kept_rows, gate_kept, up_kept = (
        partial_out.reshape(leading + (model_width,)),
        received,
        gate_pre.reshape(leading + (-1,)),
        up_pre.reshape(leading + (-1,)),
    )
    returned = lax.all_to_all(partial_out, "exp", split_axis=0, concat_axis=0, tiled=True)
    expert_out = jnp.sum(
        returned.reshape(FFN_EXPERTS, split_parts, capacity, model_width).astype(jnp.float32),
        axis=1,
    )
    position = expert_ids * capacity + slot_index
    picked = jnp.where(
        is_ffn[..., None], expert_out.reshape(-1, model_width)[jnp.where(is_ffn, position, 0)], 0.0
    )
    selected = picked + jnp.where(
        (route_ids == FFN_EXPERTS + 1)[..., None], normed_moe[:, None, :], 0.0
    )
    selected = selected + jnp.where(
        (route_ids == FFN_EXPERTS + 2)[..., None], const_out[:, 0:1], 0.0
    )
    selected = selected + jnp.where(
        (route_ids == FFN_EXPERTS + 3)[..., None], const_out[:, 1:2], 0.0
    )
    mixed_out = (hidden + jnp.sum(gate_values[..., None] * selected, axis=1)).astype(jnp.bfloat16)[
        None
    ]
    upstream = out_grad[0].astype(jnp.float32)
    d_gate_values = jnp.sum(upstream[:, None, :] * selected, axis=-1)
    weighted = gate_values[..., None] * upstream[:, None, :]
    flat_position = jnp.where(is_ffn, position, FFN_EXPERTS * capacity)
    d_expert = (
        jnp.zeros((FFN_EXPERTS * capacity, model_width), jnp.float32)
        .at[flat_position]
        .set(weighted, mode="drop")
    )
    d_expert_low = d_expert.astype(jnp.bfloat16).reshape(FFN_EXPERTS, capacity, model_width)
    incoming_grad = lax.all_to_all(
        jnp.repeat(d_expert_low, split_parts, axis=0),
        "exp",
        split_axis=0,
        concat_axis=0,
        tiled=True,
    )
    flat_rows = kept_rows.reshape(-1, model_width)
    flat_grad = incoming_grad.reshape(-1, model_width)
    gate_flat = gate_kept.reshape(flat_rows.shape[0], -1)
    up_flat = up_kept.reshape(flat_rows.shape[0], -1)
    sigmoid_gate = jax.nn.sigmoid(gate_flat)
    silu_gate = gate_flat * sigmoid_gate
    inner_act = (silu_gate * up_flat).astype(jnp.bfloat16)
    d_inner = jnp.dot(flat_grad, w_down[0].T, preferred_element_type=jnp.float32)
    d_w_down_local = jnp.dot(inner_act.T, flat_grad, preferred_element_type=jnp.float32)
    d_gate_pre = (
        d_inner * up_flat * sigmoid_gate * (1.0 + gate_flat * (1.0 - sigmoid_gate))
    ).astype(jnp.bfloat16)
    d_up_pre = (d_inner * silu_gate).astype(jnp.bfloat16)
    d_w_gate_local = jnp.dot(flat_rows.T, d_gate_pre, preferred_element_type=jnp.float32)
    d_w_up_local = jnp.dot(flat_rows.T, d_up_pre, preferred_element_type=jnp.float32)
    gate_up_local = jnp.stack([d_w_gate_local, d_w_up_local])[None]
    down_local = d_w_down_local[None]
    d_rows = jnp.dot(d_gate_pre, w_gate[0].T, preferred_element_type=jnp.float32) + jnp.dot(
        d_up_pre, w_up[0].T, preferred_element_type=jnp.float32
    )
    row_grads = lax.all_to_all(
        d_rows.reshape(kept_rows.shape).astype(jnp.bfloat16),
        "exp",
        split_axis=0,
        concat_axis=0,
        tiled=True,
    ).astype(jnp.float32)
    d_dispatch = jnp.sum(row_grads.reshape(FFN_EXPERTS, split_parts, capacity, model_width), axis=1)
    expert_sums = (
        lax.psum_scatter(
            gate_up_local.astype(jnp.bfloat16), "ctx", scatter_dimension=2, tiled=True
        ).astype(jnp.float32),
        lax.psum_scatter(
            down_local.astype(jnp.bfloat16), "ctx", scatter_dimension=1, tiled=True
        ).astype(jnp.float32),
    )
    total_gate_up = expert_sums[0][0]
    total_down = expert_sums[1][0]
    d_moe_low = (
        jnp.zeros((tok_rows + 1, model_width), jnp.float32).at[dispatch].add(d_dispatch)[:tok_rows]
    )
    onehot_routes = (route_ids[..., None] == jnp.arange(ALL_EXPERTS, dtype=jnp.int32)).astype(
        jnp.float32
    )
    d_probs = jnp.sum(onehot_routes * d_gate_values[..., None], axis=1)
    d_logits = probs_all * (d_probs - jnp.sum(probs_all * d_probs, axis=-1, keepdims=True))
    moe_wide = moe_low.astype(jnp.float32)
    d_router = jnp.dot(moe_wide.T, d_logits, precision=highest)
    d_moe_low = d_moe_low + jnp.dot(d_logits, router.astype(jnp.float32).T, precision=highest)
    const_weight = jnp.stack(
        [
            jnp.sum(jnp.where(route_ids == FFN_EXPERTS + 2 + offset, gate_values, 0.0), axis=1)
            for offset in range(2)
        ],
        axis=1,
    )
    d_const_out = const_weight[..., None] * upstream[:, None, :]
    d_alpha = jnp.stack(
        [
            jnp.sum(d_const_out * normed_moe[:, None, :], axis=-1),
            jnp.sum(d_const_out * const_vec[None], axis=-1),
        ],
        axis=-1,
    )
    d_const_logits = alphas * (d_alpha - jnp.sum(alphas * d_alpha, axis=-1, keepdims=True))
    d_const_gate = jnp.einsum("td,tca->cda", moe_wide, d_const_logits, precision=highest)
    d_moe_low = d_moe_low + jnp.einsum(
        "tca,cda->td", d_const_logits, const_gate.astype(jnp.float32), precision=highest
    )
    d_const_vec = jnp.sum(d_const_out * alphas[..., 1:2], axis=0)
    copy_weight = jnp.sum(jnp.where(route_ids == FFN_EXPERTS + 1, gate_values, 0.0), axis=1)
    d_normed = (
        d_moe_low
        + copy_weight[:, None] * upstream
        + jnp.sum(d_const_out * alphas[..., 0:1], axis=1)
    )
    d_hidden_norm, d_moe_gain = rms_backward(hidden, inverse_moe, moe_gain, d_normed)
    d_hidden = upstream + d_hidden_norm
    d_attn_low = d_hidden.astype(jnp.bfloat16)
    d_w_out = jnp.dot(mixed_low.T, d_attn_low, preferred_element_type=jnp.float32)
    d_mixed = jnp.dot(d_attn_low, w_out.T, preferred_element_type=jnp.float32).astype(jnp.bfloat16)
    kv_back = lax.all_gather(kv_local, "ctx", axis=0, tiled=True)
    all_back = jnp.concatenate([kv_back, own_kv], axis=0)
    d_heads = lax.map(
        partial(head_backward, allowed),
        (
            split_heads(queries),
            split_heads(all_back[:, :model_width]),
            split_heads(all_back[:, model_width:]),
            split_heads(d_mixed),
            row_lse,
        ),
    )
    d_queries = join_heads(d_heads[0])
    kv_grad = jnp.concatenate([join_heads(d_heads[1]), join_heads(d_heads[2])], axis=-1)
    own_prompt_grad = lax.psum_scatter(
        kv_grad[:prompt_len].astype(jnp.bfloat16), "ctx", scatter_dimension=0, tiled=True
    ).astype(jnp.float32)
    kv_rows = jnp.concatenate([own_prompt_grad, kv_grad[prompt_len:]], axis=0)
    d_projected = jnp.concatenate([d_queries, kv_rows], axis=-1).astype(jnp.bfloat16)
    d_w_qkv = jnp.dot(act_low.T, d_projected, preferred_element_type=jnp.float32)
    d_act = jnp.dot(d_projected, w_qkv.T, preferred_element_type=jnp.float32)
    d_tokens_norm, d_attn_gain = rms_backward(tokens_in, inverse_attn, attn_gain, d_act)
    d_inputs = (d_hidden + d_tokens_norm)[None]
    dense_sums = lax.psum(
        (d_attn_gain, d_w_qkv, d_w_out, d_moe_gain, d_router, d_const_gate, d_const_vec),
        ("ctx", "exp"),
    )
    return (
        mixed_out,
        d_inputs,
        d_logits[None],
        dense_sums[0],
        dense_sums[1],
        dense_sums[2],
        dense_sums[3],
        dense_sums[4],
        dense_sums[5],
        dense_sums[6],
        total_gate_up[0][None],
        total_gate_up[1][None],
        total_down[None],
    )


def solution(mesh):
    return jax.shard_map(
        body,
        mesh=mesh,
        in_specs=(
            P("ctx", "exp", None),
            P("ctx", "exp", None),
            P("ctx", "exp", None),
            P(),
            P(),
            P(),
            P(),
            P(),
            P(),
            P(),
            P("exp", None, None),
            P("exp", None, None),
            P("exp", None, None),
            P("ctx", "exp", None),
        ),
        out_specs=(
            P("ctx", "exp", None),
            P("ctx", "exp", None),
            P("ctx", "exp", None),
            P(),
            P(),
            P(),
            P(),
            P(),
            P(),
            P(),
            P("exp", "ctx", None),
            P("exp", "ctx", None),
            P("exp", "ctx", None),
        ),
        check_vma=False,
    )
```

profile of v0, /device:TPU:0, one launch (start us, length us, event | category | flops | bytes accessed | tf_op | source)
XLA Modules:
  0.0 1069.1 jit_solution(18259728918760266135)
XLA Ops:
  26.2 7.3 reduce-window.6
  91.6 130.8 %while.28 = (s32[]{:T(128)}, bf16[12,768,64]{1,2,0:T(8,128)(2,1)}, f32[12,768]{1,0:T(8,128)}, bf16[12,768,64]{2,1,0:T(8,128)(2,1)}, bf16[12,1536,64]{2,1,0:T(8,1...) while((s32[]{:T(128)}, bf16[12,768,64]{1,2,0:T(8,128)(2,1)}, ...), condition=%wide.region_4.5_spmd.clone, body=%wide.region_1.4_spmd.clone.sunk | while | flops 317324544 | bytes 34315476 | solution.py:125
  230.3 7.2 gather_fusion
  252.5 11.5 %gather_fusion.2 = f32[1536]{0:T(1024)S(1)} fusion(f32[768,12]{0,1:T(8,128)} %fusion.115, s32[1536]{0:T(1024)S(1)} %reshape.454), kind=kCustom, calls=%fused_computation.2 | custom fusion | bytes 24576 | tf_op jit(solution)/shard_map/jit(take_along_axis)/gather | solution.py:140
  282.4 9.7 scatter_custom_fusion
  313.2 10.1 fusion.65
  323.3 7.7 fusion.69
  331.0 12.1 %all-to-all-done.2 = bf16[8,144,768]{2,1,0:T(8,128)(2,1)} async-done(((bf16[8,144,768]{2,1,0:T(8,128)(2,1)}), bf16[8,144,768]{2,1,0:T(8,128)(2,1)}, u32[]{:S(2)}, u32[]{:S(2)}) %all-to-all-start.2) | async-done | bytes 1769504 | tf_op jit(solution)/shard_map/all_to_all | solution.py:205
  343.1 16.6 %multiply_convert_fusion.1 = (bf16[1152,2048]{1,0:T(8,128)(2,1)}, bf16[1152,2048]{1,0:T(8,128)(2,1)}, bf16[1152,2048]{1,0:T(8,128)(2,1)}) fusion(f32[1152,2048]{1,0:T(8,128)} %fusion.69, f32[1152,2048]{1,0:T(8,128)} %fusion.65, bf16[1152,768]{1,0:T(8,128)(2,1)} %bitcast.27, bf16[1,2048,768]{2,1,0:T(8,128)(2,1)} %param.30), kind=kOutput, calls=%fused_computation.66 | convolution fusion | flops 3659268096 | bytes 37945344 | tf_op jit(solution)/shard_map/dot_general | solution.py:219
  359.7 7.4 convolution_convert_fusion.4
  395.8 7.5 fusion.60
  403.3 10.5 all-to-all-done.1
  421.9 8.9 gather_fusion.1
  437.4 38.7 %fusion.57 = (f32[2,768]{1,0:T(2,128)}, f32[768,768]{1,0:T(8,128)}, f32[768,2]{1,0:T(8,128)}, f32[768,2]{1,0:T(8,128)}, f32[768,768]{1,0:T(8,128)}, /*index=5*/f32[768,2]{1,0:T(8,128)}) fusion(f32[768,2]{1,0:T(8,128)} %copy.148, f32[768,768]{1,0:T(8,128)} %bitcast_convert_fusion.1, f32[768,2]{1,0:T(8,128)} %bitcast.275, f32[768,2]{1,0:T(8,128)} %bitcast.273, ...), kind=kLoop, calls=%fused_computation.86 | loop fusion | flops 22407168 | bytes 18935808 | tf_op jit(solution)/shard_map/reduce_sum | solution.py:281
  488.5 13.2 %scatter_custom_fusion.1 = f32[769,768]{1,0:T(8,128)} fusion(s32[1152]{0:T(1024)} %copy-done.33, bf16[1152,768]{1,0:T(8,128)(2,1)} %bitcast.65, f32[]{:T(128)} %constant.56.clone.1), kind=kCustom, calls=%fused_computation.95 | custom fusion | flops 1769472 | bytes 4132352 | tf_op jit(solution)/shard_map/scatter-add | solution.py:251
  517.6 168.1 %while.29 = (s32[]{:T(128)}, bf16[12,768,64]{1,2,0:T(8,128)(2,1)}, bf16[12,1536,64]{1,2,0:T(8,128)(2,1)}, bf16[12,1536,64]{1,2,0:T(8,128)(2,1)}, bf16[12,768,64]...) while((s32[]{:T(128)}, bf16[12,768,64]{1,2,0:T(8,128)(2,1)}, ...), condition=%wide.region_30.31_spmd.clone, body=%wide.region_28.30_spmd.clone.sunk | while | flops 772816128 | bytes 38401196 | solution.py:295
  690.7 8.9 fusion.73
  706.8 7.4 fusion.72
  723.0 12.9 %reduce-scatter.4.cloned.1.call-done = bf16[256,1536]{0,1:T(8,128)(2,1)} async-done(((bf16[1024,1536]{0,1:T(8,128)(2,1)}), bf16[256,1536]{0,1:T(8,128)(2,1)}) %reduce-scatter.4.cloned.1.call-update) | async-done | bytes 786448 | tf_op jit(solution)/shard_map/reduce_scatter | solution.py:307
  735.9 8.5 fusion.90
  750.9 31.9 %reduce-scatter.8.cloned.1.call-done = bf16[1,512,768]{2,1,0:T(8,128)(2,1)} async-done(((bf16[1,2048,768]{2,1,0:T(8,128)(2,1)}), bf16[1,512,768]{2,1,0:T(8,128)(2,1)}) %reduce-scatter.8.cloned.1.call-update) | async-done | bytes 786448 | tf_op jit(solution)/shard_map/reduce_scatter | solution.py:244
  792.3 41.7 %all-reduce.1 = (f32[768]{0:T(1024)}, f32[768]{0:T(1024)}, f32[768,12]{0,1:T(8,128)}, f32[2,768,2]{1,2,0:T(2,128)}, f32[2,768]{1,0:T(2,128)}) all-reduce(f32[768]{0:T(1024)} %get-tuple-element.381, f32[768]{0:T(1024)} %get-tuple-element.377, f32[768,12]{0,1:T(8,128)} %fusion.130, ...), channel_id=1, replica_groups=mesh['ctx'=4,'exp'=8] {'ctx','exp'}, use_global_device_ids=true, to_apply=%region_34.35 | all-reduce | flops 15360 | bytes 122880 | tf_op jit(solution)/shard_map/psum | solution.py:316
  840.5 16.3 %reduce-scatter.6.cloned.1.call-done = bf16[1,2,192,2048]{3,2,1,0:T(8,128)(2,1)} async-done(((bf16[1,2,768,2048]{3,2,1,0:T(8,128)(2,1)}), bf16[1,2,192,2048]{3,2,1,0:T(8,128)(2,1)}) %reduce-scatter.6.cloned.1.call-update) | async-done | bytes 1572880 | tf_op jit(solution)/shard_map/reduce_scatter | solution.py:241
  860.4 194.0 %all-reduce.5.cloned.1.call-done = (f32[768,2304]{1,0:T(8,128)}, f32[768,768]{1,0:T(8,128)}) async-done(((f32[768,2304]{1,0:T(8,128)}, f32[768,768]{1,0:T(8,128)}), (f32[768,2304]{1,0:T(8,128)}, f32[768,768]{1,0:T(8,128)})) %all-reduce.5.cloned.1.call-update) | async-done | bytes 9437200 | tf_op jit(solution)/shard_map/psum | solution.py:316
  (474 shorter events, 564.1 us)
Async XLA Ops:
  7.2 58.8 %all-gather.2.cloned.1.call-start = ((), (), s32[]{:S(2)}) async-start(), calls=%async_computation.7 | async-start | bytes 3932160 | tf_op jit(solution)/shard_map/all_gather | solution.py:115
  57.5 7.3 copy-start.33
  237.4 58.0 %all-to-all-start = ((bf16[8,144,768]{2,1,0:T(8,128)(2,1)}), bf16[8,144,768]{2,1,0:T(8,128)(2,1)}, u32[]{:S(2)}, u32[]{:S(2)}) async-start(bf16[8,144,768]{2,1,0:T(8,128)(2,1)} %bitcast.269), calls=%async_computation | async-start | bytes 3538944 | tf_op jit(solution)/shard_map/all_to_all | solution.py:157
  295.4 47.7 %all-to-all-start.2 = ((bf16[8,144,768]{2,1,0:T(8,128)(2,1)}), bf16[8,144,768]{2,1,0:T(8,128)(2,1)}, u32[]{:S(2)}, u32[]{:S(2)}) async-start(bf16[8,144,768]{2,1,0:T(8,128)(2,1)} %bitcast.270), calls=%async_computation.2 | async-start | bytes 3538944 | tf_op jit(solution)/shard_map/all_to_all | solution.py:205
  308.0 15.3 %copy-start.28 = (f32[768,2]{0,1:T(2,128)}, f32[768,2]{0,1:T(2,128)S(1)}, u32[]{:S(2)}) copy-start(f32[768,2]{0,1:T(2,128)S(1)} %get-tuple-element.485) | copy-start | bytes 18436
  313.2 10.1 copy-start.47
  343.1 16.6 %copy-start.46 = (bf16[1,2048,768]{2,1,0:T(8,128)(2,1)S(1)}, bf16[1,2048,768]{2,1,0:T(8,128)(2,1)}, u32[]{:S(2)}) copy-start(bf16[1,2048,768]{2,1,0:T(8,128)(2,1)} %param.30) | copy-start | bytes 9437188
  367.1 46.7 %all-to-all-start.1 = ((bf16[8,144,768]{2,1,0:T(8,128)(2,1)}), bf16[8,144,768]{2,1,0:T(8,128)(2,1)}, u32[]{:S(2)}, u32[]{:S(2)}) async-start(bf16[8,144,768]{2,1,0:T(8,128)(2,1)} %bitcast.277), calls=%async_computation.1 | async-start | bytes 3538944 | tf_op jit(solution)/shard_map/all_to_all | solution.py:174
  413.8 74.7 %all-to-all-start.3 = ((bf16[8,144,768]{2,1,0:T(8,128)(2,1)}), bf16[8,144,768]{2,1,0:T(8,128)(2,1)}, u32[]{:S(2)}, u32[]{:S(2)}) async-start(bf16[8,144,768]{2,1,0:T(8,128)(2,1)} %bitcast.276), calls=%async_computation.3 | async-start | bytes 3538944 | tf_op jit(solution)/shard_map/all_to_all | solution.py:232
  418.1 317.8 %reduce-scatter.4.cloned.1.call-start = ((), (), s32[]{:S(2)}) async-start(), calls=%async_computation.8 | async-start | bytes 3932160 | tf_op jit(solution)/shard_map/reduce_scatter | solution.py:307
  437.4 45.5 %copy-start.21 = (f32[768]{0:T(1024)S(1)}, f32[768]{0:T(1024)}, u32[]{:S(2)}) copy-start(f32[768]{0:T(1024)} %copy-done.20) | copy-start | bytes 9220
  437.4 47.8 %copy-start.19 = (f32[768,2,2]{0,2,1:T(2,128)S(1)}, f32[768,2,2]{0,2,1:T(2,128)}, u32[]{:S(2)}) copy-start(f32[768,2,2]{0,2,1:T(2,128)} %copy-done.18) | copy-start | bytes 36868
  488.5 13.2 %copy-start.26 = (f32[768]{0:T(1024)S(1)}, f32[768]{0:T(1024)}, u32[]{:S(2)}) copy-start(f32[768]{0:T(1024)} %copy-done.25) | copy-start | bytes 9220
  501.7 7.1 copy-start.5
  501.8 7.1 copy-start.6
  501.8 7.0 copy-start.10
  501.8 7.0 copy-start.31
  501.8 7.0 copy-start.38
  690.4 92.4 %reduce-scatter.8.cloned.1.call-start = ((), (), s32[]{:S(2)}) async-start(), calls=%async_computation.10 | async-start | bytes 3932160 | tf_op jit(solution)/shard_map/reduce_scatter | solution.py:244
  699.6 157.2 %reduce-scatter.6.cloned.1.call-start = ((), (), s32[]{:S(2)}) async-start(), calls=%async_computation.9 | async-start | bytes 7864320 | tf_op jit(solution)/shard_map/reduce_scatter | solution.py:241
  717.4 337.0 %all-reduce.5.cloned.1.call-start = ((), (), s32[]{:S(2)}) async-start(), calls=%async_computation.11 | async-start | bytes 18874368 | tf_op jit(solution)/shard_map/psum | solution.py:316
  720.5 15.4 %copy-start.37 = (f32[768]{0:T(1024)S(1)}, f32[768]{0:T(1024)}, u32[]{:S(2)}) copy-start(f32[768]{0:T(1024)} %copy-done.36) | copy-start | bytes 9220
  785.4 6.9 copy-start.29
  785.4 49.4 %copy-start.35 = (f32[768]{0:T(1024)S(1)}, f32[768]{0:T(1024)}, u32[]{:S(2)}) copy-start(f32[768]{0:T(1024)} %get-tuple-element.477) | copy-start | bytes 9220
  (79 other events, 225.5 us)
Sparse Core Ops, SparseCore 0:
  17.3 46.6 all-gather.1
  690.6 45.2 reduce-scatter.3
  738.9 43.9 reduce-scatter.7
  785.7 71.0 reduce-scatter.5
  863.2 191.2 all-reduce.4
where the time goes:
time: 1080 us; the launch traced here: 1070 us
  matrix products  367 us (34%)
  waiting for transfers between devices  278 us (26%)
  local copies, waits for them, and re-layouts  200 us (19%)
  other arithmetic  146 us (14%)
  blocking collectives  41.7 us (4%)
  starting transfers between devices  21.9 us (2%)
  between operations  14.5 us (1%)
    psum x1, waiting for transfers between devices, body(): lax.psum((d_attn_gain, d_w_qkv, d_w_out, d_moe_gain, d_router, d_const_ga...  194 us
    dot_general x12, matrix products, head_forward(): jnp.einsum('qk,kd->qd', weights_soft, value_rows, preferred_element_type=...  50.2 us
    dot_general x12, matrix products, head_backward(): jnp.einsum('qd,kd->qk', queries, key_rows, preferred_element_type=jnp.flo...  48.2 us
    unnamed x106, local copies, waits for them, and re-layouts  45.2 us
    psum x1, blocking collectives, body(): lax.psum((d_attn_gain, d_w_qkv, d_w_out, d_moe_gain, d_router, d_const_ga...  41.7 us
    reduce_sum x1, other arithmetic, body(): d_const_vec = jnp.sum(d_const_out * alphas[..., 1:2], axis=0)  38.7 us
    dot_general x12, matrix products, head_forward(): jnp.einsum('qd,kd->qk', queries, key_rows, preferred_element_type=jnp.flo...  38.3 us
    reduce_scatter x1, waiting for transfers between devices, body(): lax.psum_scatter(down_local.astype(jnp.bfloat16), 'ctx', scatter_dimensio...  31.9 us
  transfers between devices with their start and end apart: 9, of which 6 were waited for; matrix products, arithmetic and copies ran while one was open for 28% of the time, Pallas kernels for 0%

commit v1 on v0

--- a/solution.py
+++ b/solution.py
@@ -313,10 +313,10 @@
     d_act = jnp.dot(d_projected, w_qkv.T, preferred_element_type=jnp.float32)
     d_tokens_norm, d_attn_gain = rms_backward(tokens_in, inverse_attn, attn_gain, d_act)
     d_inputs = (d_hidden + d_tokens_norm)[None]
-    dense_sums = lax.psum(
-        (d_attn_gain, d_w_qkv, d_w_out, d_moe_gain, d_router, d_const_gate, d_const_vec),
-        ("ctx", "exp"),
-    )
+    one_axis = lax.psum(
+        (d_attn_gain, d_w_qkv, d_w_out, d_moe_gain, d_router, d_const_gate, d_const_vec), "exp"
+    )
+    dense_sums = lax.psum(one_axis, "ctx")
     return (
         mixed_out,
         d_inputs,

time: 1080 us -> 1280 us (1.19)
  waiting for transfers between devices: 278 us -> 471 us
    psum x0 -> x1, waiting for transfers between devices: none -> 189 us  [body(): dense_sums = lax.psum(one_axis, 'ctx')]
    reduce_scatter x1, waiting for transfers between devices: 12.9 us -> 39.9 us  [body(): lax.psum_scatter(kv_grad[:prompt_len].astype(jnp.bfloat16), 'ctx', scatte...]
    psum x1, waiting for transfers between devices: 194 us -> 169 us  [body(): lax.psum((d_attn_gain, d_w_qkv, d_w_out, d_moe_gain, d_router, d_const_ga...]
    psum x0 -> x1, blocking collectives: none -> 17.7 us  [body(): dense_sums = lax.psum(one_axis, 'ctx')]
  transfers between devices with their start and end apart: 9 -> 10, of which waited for: 6 -> 7; matrix products, arithmetic and copies ran while one was open for 28% -> 23% of each run, Pallas kernels for 0% -> 0%
where the time goes in v1:
time: 1280 us; the launch traced here: 1270 us
  waiting for transfers between devices  471 us (37%)
  matrix products  367 us (29%)
  local copies, waits for them, and re-layouts  200 us (16%)
  other arithmetic  145 us (11%)
  blocking collectives  48.5 us (4%)
  starting transfers between devices  22.2 us (2%)
  between operations  14.9 us (1%)
    psum x1, waiting for transfers between devices, body(): dense_sums = lax.psum(one_axis, 'ctx')  189 us
    psum x1, waiting for transfers between devices, body(): lax.psum((d_attn_gain, d_w_qkv, d_w_out, d_moe_gain, d_router, d_const_ga...  169 us
    dot_general x12, matrix products, head_forward(): jnp.einsum('qk,kd->qd', weights_soft, value_rows, preferred_element_type=...  50.2 us
    dot_general x12, matrix products, head_backward(): jnp.einsum('qd,kd->qk', queries, key_rows, preferred_element_type=jnp.flo...  48.2 us
    unnamed x106, local copies, waits for them, and re-layouts  45.2 us
    reduce_scatter x1, waiting for transfers between devices, body(): lax.psum_scatter(down_local.astype(jnp.bfloat16), 'ctx', scatter_dimensio...  40.5 us
    reduce_scatter x1, waiting for transfers between devices, body(): lax.psum_scatter(kv_grad[:prompt_len].astype(jnp.bfloat16), 'ctx', scatte...  39.9 us
    reduce_sum x1, other arithmetic, body(): d_const_vec = jnp.sum(d_const_out * alphas[..., 1:2], axis=0)  38.7 us
  transfers between devices with their start and end apart: 10, of which 7 were waited for; matrix products, arithmetic and copies ran while one was open for 23% of the time, Pallas kernels for 0%

profile of v1, /device:TPU:0, one launch (start us, length us, event | category | flops | bytes accessed | tf_op | source)
XLA Modules:
  0.0 1268.9 jit_solution(6101374258671898628)
XLA Ops:
  26.2 7.3 reduce-window.6
  91.6 130.8 %while.28 = (s32[]{:T(128)}, bf16[12,768,64]{1,2,0:T(8,128)(2,1)}, f32[12,768]{1,0:T(8,128)}, bf16[12,768,64]{2,1,0:T(8,128)(2,1)}, bf16[12,1536,64]{2,1,0:T(8,1...) while((s32[]{:T(128)}, bf16[12,768,64]{1,2,0:T(8,128)(2,1)}, ...), condition=%wide.region_4.5_spmd.clone, body=%wide.region_1.4_spmd.clone.sunk | while | flops 317324544 | bytes 34315476 | solution.py:125
  252.5 11.5 gather_fusion.2
  282.4 9.7 scatter_custom_fusion
  313.2 10.1 fusion.65
  323.3 7.7 fusion.69
  331.0 12.1 all-to-all-done.2
  343.1 16.6 %multiply_convert_fusion.1 = (bf16[1152,2048]{1,0:T(8,128)(2,1)}, bf16[1152,2048]{1,0:T(8,128)(2,1)}, bf16[1152,2048]{1,0:T(8,128)(2,1)}) fusion(f32[1152,2048]{1,0:T(8,128)} %fusion.69, f32[1152,2048]{1,0:T(8,128)} %fusion.65, bf16[1152,768]{1,0:T(8,128)(2,1)} %bitcast.27, bf16[1,2048,768]{2,1,0:T(8,128)(2,1)} %param.30), kind=kOutput, calls=%fused_computation.66 | convolution fusion | flops 3659268096 | bytes 37945344 | tf_op jit(solution)/shard_map/dot_general | solution.py:219
  359.7 7.4 convolution_convert_fusion.4
  395.8 7.5 fusion.60
  403.3 10.5 all-to-all-done.1
  421.9 8.9 gather_fusion.1
  437.4 38.7 %fusion.57 = (f32[2,768]{1,0:T(2,128)}, f32[768,768]{1,0:T(8,128)}, f32[768,2]{1,0:T(8,128)}, f32[768,2]{1,0:T(8,128)}, f32[768,768]{1,0:T(8,128)}, /*index=5*/f32[768,2]{1,0:T(8,128)}) fusion(f32[768,2]{1,0:T(8,128)} %copy.148, f32[768,768]{1,0:T(8,128)} %bitcast_convert_fusion.1, f32[768,2]{1,0:T(8,128)} %bitcast.275, f32[768,2]{1,0:T(8,128)} %bitcast.273, ...), kind=kLoop, calls=%fused_computation.86 | loop fusion | flops 22407168 | bytes 18935808 | tf_op jit(solution)/shard_map/reduce_sum | solution.py:281
  488.5 13.2 %scatter_custom_fusion.1 = f32[769,768]{1,0:T(8,128)} fusion(s32[1152]{0:T(1024)} %copy-done.33, bf16[1152,768]{1,0:T(8,128)(2,1)} %bitcast.65, f32[]{:T(128)} %constant.56.clone.1), kind=kCustom, calls=%fused_computation.95 | custom fusion | flops 1769472 | bytes 4132352 | tf_op jit(solution)/shard_map/scatter-add | solution.py:251
  517.6 168.1 %while.29 = (s32[]{:T(128)}, bf16[12,768,64]{1,2,0:T(8,128)(2,1)}, bf16[12,1536,64]{1,2,0:T(8,128)(2,1)}, bf16[12,1536,64]{1,2,0:T(8,128)(2,1)}, bf16[12,768,64]...) while((s32[]{:T(128)}, bf16[12,768,64]{1,2,0:T(8,128)(2,1)}, ...), condition=%wide.region_30.31_spmd.clone, body=%wide.region_28.30_spmd.clone.sunk | while | flops 772816128 | bytes 38401196 | solution.py:295
  696.0 39.9 %reduce-scatter.4.cloned.1.call-done = bf16[256,1536]{0,1:T(8,128)(2,1)} async-done(((bf16[1024,1536]{0,1:T(8,128)(2,1)}), bf16[256,1536]{0,1:T(8,128)(2,1)}) %reduce-scatter.4.cloned.1.call-update) | async-done | bytes 786448 | tf_op jit(solution)/shard_map/reduce_scatter | solution.py:307
  735.9 8.5 fusion.90
  744.5 8.9 fusion.73
  771.6 168.7 %all-reduce.8.cloned.1.call-done = (f32[768,2304]{1,0:T(8,128)}, f32[768,768]{1,0:T(8,128)}) async-done(((f32[768,2304]{1,0:T(8,128)}, f32[768,768]{1,0:T(8,128)}), (f32[768,2304]{1,0:T(8,128)}, f32[768,768]{1,0:T(8,128)})) %all-reduce.8.cloned.1.call-update) | async-done | bytes 9437200 | tf_op jit(solution)/shard_map/psum | solution.py:316
  946.8 40.5 %reduce-scatter.8.cloned.1.call-done = bf16[1,512,768]{2,1,0:T(8,128)(2,1)} async-done(((bf16[1,2048,768]{2,1,0:T(8,128)(2,1)}), bf16[1,512,768]{2,1,0:T(8,128)(2,1)}) %reduce-scatter.8.cloned.1.call-update) | async-done | bytes 786448 | tf_op jit(solution)/shard_map/reduce_scatter | solution.py:244
  996.7 30.8 %all-reduce.1 = (f32[768]{0:T(1024)}, f32[768]{0:T(1024)}, f32[768,12]{0,1:T(8,128)}, f32[2,768,2]{1,2,0:T(2,128)}, f32[2,768]{1,0:T(2,128)}) all-reduce(f32[768]{0:T(1024)} %get-tuple-element.381, f32[768]{0:T(1024)} %get-tuple-element.377, f32[768,12]{0,1:T(8,128)} %fusion.130, ...), channel_id=1, replica_groups=mesh['ctx'=4,'exp'=8] {'exp'}, use_global_device_ids=true, to_apply=%region_34.35 | all-reduce | flops 15360 | bytes 122880 | tf_op jit(solution)/shard_map/psum | solution.py:316
  1027.5 17.7 %all-reduce.3 = (f32[768]{0:T(1024)}, f32[768]{0:T(1024)}, f32[768,12]{0,1:T(8,128)}, f32[2,768,2]{1,2,0:T(2,128)}, f32[2,768]{1,0:T(2,128)}) all-reduce(f32[768]{0:T(1024)} %get-tuple-element.442, f32[768]{0:T(1024)} %get-tuple-element.443, f32[768,12]{0,1:T(8,128)} %get-tuple-element.444, ...), channel_id=1, replica_groups=mesh['ctx'=4,'exp'=8] {'ctx'}, use_global_device_ids=true, to_apply=%region_35.36 | all-reduce | flops 15360 | bytes 122880 | tf_op jit(solution)/shard_map/psum | solution.py:319
  1050.6 10.5 reduce-scatter.6.cloned.1.call-done
  1064.8 189.0 %all-reduce.10.cloned.1.call-done = (f32[768,2304]{1,0:T(8,128)}, f32[768,768]{1,0:T(8,128)}) async-done(((f32[768,2304]{1,0:T(8,128)}, f32[768,768]{1,0:T(8,128)}), (f32[768,2304]{1,0:T(8,128)}, f32[768,768]{1,0:T(8,128)})) %all-reduce.10.cloned.1.call-update) | async-done | bytes 9437200 | tf_op jit(solution)/shard_map/psum | solution.py:319
  (478 shorter events, 577.7 us)
Async XLA Ops:
  7.2 58.8 %all-gather.2.cloned.1.call-start = ((), (), s32[]{:S(2)}) async-start(), calls=%async_computation.7 | async-start | bytes 3932160 | tf_op jit(solution)/shard_map/all_gather | solution.py:115
  57.5 7.3 copy-start.33
  237.5 58.0 %all-to-all-start = ((bf16[8,144,768]{2,1,0:T(8,128)(2,1)}), bf16[8,144,768]{2,1,0:T(8,128)(2,1)}, u32[]{:S(2)}, u32[]{:S(2)}) async-start(bf16[8,144,768]{2,1,0:T(8,128)(2,1)} %bitcast.269), calls=%async_computation | async-start | bytes 3538944 | tf_op jit(solution)/shard_map/all_to_all | solution.py:157
  295.4 47.7 %all-to-all-start.2 = ((bf16[8,144,768]{2,1,0:T(8,128)(2,1)}), bf16[8,144,768]{2,1,0:T(8,128)(2,1)}, u32[]{:S(2)}, u32[]{:S(2)}) async-start(bf16[8,144,768]{2,1,0:T(8,128)(2,1)} %bitcast.270), calls=%async_computation.2 | async-start | bytes 3538944 | tf_op jit(solution)/shard_map/all_to_all | solution.py:205
  308.0 15.3 %copy-start.28 = (f32[768,2]{0,1:T(2,128)}, f32[768,2]{0,1:T(2,128)S(1)}, u32[]{:S(2)}) copy-start(f32[768,2]{0,1:T(2,128)S(1)} %get-tuple-element.492) | copy-start | bytes 18436
  313.2 10.1 copy-start.47
  343.1 16.6 %copy-start.46 = (bf16[1,2048,768]{2,1,0:T(8,128)(2,1)S(1)}, bf16[1,2048,768]{2,1,0:T(8,128)(2,1)}, u32[]{:S(2)}) copy-start(bf16[1,2048,768]{2,1,0:T(8,128)(2,1)} %param.30) | copy-start | bytes 9437188
  367.1 46.7 %all-to-all-start.1 = ((bf16[8,144,768]{2,1,0:T(8,128)(2,1)}), bf16[8,144,768]{2,1,0:T(8,128)(2,1)}, u32[]{:S(2)}, u32[]{:S(2)}) async-start(bf16[8,144,768]{2,1,0:T(8,128)(2,1)} %bitcast.277), calls=%async_computation.1 | async-start | bytes 3538944 | tf_op jit(solution)/shard_map/all_to_all | solution.py:174
  413.8 74.7 %all-to-all-start.3 = ((bf16[8,144,768]{2,1,0:T(8,128)(2,1)}), bf16[8,144,768]{2,1,0:T(8,128)(2,1)}, u32[]{:S(2)}, u32[]{:S(2)}) async-start(bf16[8,144,768]{2,1,0:T(8,128)(2,1)} %bitcast.276), calls=%async_computation.3 | async-start | bytes 3538944 | tf_op jit(solution)/shard_map/all_to_all | solution.py:232
  418.1 317.8 %reduce-scatter.4.cloned.1.call-start = ((), (), s32[]{:S(2)}) async-start(), calls=%async_computation.8 | async-start | bytes 3932160 | tf_op jit(solution)/shard_map/reduce_scatter | solution.py:307
  437.4 45.5 %copy-start.21 = (f32[768]{0:T(1024)S(1)}, f32[768]{0:T(1024)}, u32[]{:S(2)}) copy-start(f32[768]{0:T(1024)} %copy-done.20) | copy-start | bytes 9220
  437.4 47.8 %copy-start.19 = (f32[768,2,2]{0,2,1:T(2,128)S(1)}, f32[768,2,2]{0,2,1:T(2,128)}, u32[]{:S(2)}) copy-start(f32[768,2,2]{0,2,1:T(2,128)} %copy-done.18) | copy-start | bytes 36868
  488.5 13.2 %copy-start.26 = (f32[768]{0:T(1024)S(1)}, f32[768]{0:T(1024)}, u32[]{:S(2)}) copy-start(f32[768]{0:T(1024)} %copy-done.25) | copy-start | bytes 9220
  501.7 7.1 copy-start.5
  501.8 7.1 copy-start.6
  501.8 7.0 copy-start.10
  501.8 7.0 copy-start.31
  501.8 7.0 copy-start.38
  690.4 249.8 %all-reduce.8.cloned.1.call-start = ((), (), s32[]{:S(2)}) async-start(), calls=%async_computation.11 | async-start | bytes 18874368 | tf_op jit(solution)/shard_map/psum | solution.py:316
  693.5 42.4 %copy-start.37 = (f32[768]{0:T(1024)S(1)}, f32[768]{0:T(1024)}, u32[]{:S(2)}) copy-start(f32[768]{0:T(1024)} %copy-done.36) | copy-start | bytes 9220
  744.4 242.8 %reduce-scatter.8.cloned.1.call-start = ((), (), s32[]{:S(2)}) async-start(), calls=%async_computation.10 | async-start | bytes 3932160 | tf_op jit(solution)/shard_map/reduce_scatter | solution.py:244
  753.5 307.7 %reduce-scatter.6.cloned.1.call-start = ((), (), s32[]{:S(2)}) async-start(), calls=%async_computation.9 | async-start | bytes 7864320 | tf_op jit(solution)/shard_map/reduce_scatter | solution.py:241
  771.3 482.5 %all-reduce.10.cloned.1.call-start = ((), (), s32[]{:S(2)}) async-start(), calls=%async_computation.12 | async-start | bytes 18874368 | tf_op jit(solution)/shard_map/psum | solution.py:319
  989.8 56.1 %copy-start.35 = (f32[768]{0:T(1024)S(1)}, f32[768]{0:T(1024)}, u32[]{:S(2)}) copy-start(f32[768]{0:T(1024)} %get-tuple-element.484) | copy-start | bytes 9220
  (80 other events, 232.4 us)
Sparse Core Ops, SparseCore 0:
  17.3 46.6 all-gather.1
  690.6 45.2 reduce-scatter.3
  744.6 195.6 all-reduce.7
  943.1 44.0 reduce-scatter.7
  990.0 71.0 reduce-scatter.5
  1064.7 189.0 all-reduce.9
